TPU v7x, 32 devices: a whole 2x2x4 slice. The times are simulated.
32 devices in a mesh: sub: 8 (over y, x, core), front: 4 (over z).
Axes of the slice: x: 2, y: 2, z: 4, core: 2. Of those that a mesh axis runs over, the one named last changes fastest.
Arguments:
- front_inverse: bfloat16 [8, 8192, 2048], P('sub', 'front'), may hold values from -0.75 to 0.75
- coupling: bfloat16 [8, 8192, 2048], P('sub', 'front'), may hold values from -0.0234375 to 0.0234375
- free_modes: bfloat16 [8, 300, 8192], P('sub', None, 'front'), may hold values from -0.125 to 0.125
- dof_offset: int32 [8, 256], P('sub', 'front'), may hold values from 0 to 2047, as said below
- interface_id: int32 [8, 256], replicated, may hold values from 0 to 1023, as said below
Outputs:
- attachment: bfloat16 [8, 256, 8192], P('sub', None, 'front')
- flexibility: float32 [1024, 1024], P(('sub', 'front'))
Inputs may be any that keep to these rules, and one draw needn't show every extreme that they name: `dof_offset`: within one substructure and one front the 64 offsets are distinct, and 0 and 2047 occur among them. `interface_id`: every value occurs exactly twice in the whole array.
All inputs are finite; a program needn't handle non-finite values.
Results may differ from a plain program's by a relative error of at most 0.02.
Values may be sent and summed in bfloat16 or wider, within the bound.
No kernel may reach another device: no remote copies, remote signals or barrier semaphores. Data moves between devices by JAX's collectives and lax.ppermute only.
A program may use at most 128 MiB of HBM per device.

v0:
```python
import jax
import jax.numpy as jnp
from jax import lax
from jax.sharding import PartitionSpec as P


def shifted(value, axis, steps):
    count = lax.axis_size(axis)
    leading, last = (max(0, -steps), min(count, count - steps))
    return lax.ppermute(value, axis, [(source, source + steps) for source in range(leading, last)])


def contract_last(left, right):
    return lax.dot_general(
        left, right, (((1,), (1,)), ((), ())), preferred_element_type=jnp.float32
    )


def on_device(front_inverse, coupling, free_modes, dof_offset, interface_id):
    inverse_block = front_inverse[0]
    coupling_block = coupling[0]
    mode_block = free_modes[0]
    offsets = dof_offset[0]
    order = inverse_block.shape[0]
    columns_all = interface_id.shape[1]
    per_front = offsets.shape[0]
    fronts = lax.axis_size("front")
    front_pos = lax.axis_index("front")
    sub_pos = lax.axis_index("sub")
    column_ids = jnp.arange(columns_all, dtype=jnp.int32)
    local_ids = jnp.arange(per_front, dtype=jnp.int32)
    row_ids = jnp.arange(order, dtype=jnp.int32)
    column_pick = (column_ids[:, None] == front_pos * per_front + local_ids[None, :]).astype(
        jnp.float32
    )
    row_pick = (offsets[:, None] == row_ids[None, :]).astype(jnp.float32)
    forces = jnp.dot(column_pick, row_pick, precision=lax.Precision.HIGHEST)
    groups = 1
    width = columns_all // groups
    force_groups = forces.reshape(groups, width, order)
    moments = groups + fronts - 1

    def forward(moment, carry):
        solved, outgoing = carry
        incoming = shifted(outgoing, "front", 1)
        panel = moment - front_pos
        valid = (panel >= 0) & (panel < groups)
        clipped = jnp.clip(panel, 0, groups - 1)

        def forward_active(unused):
            load = lax.dynamic_index_in_dim(force_groups, clipped, 0, keepdims=False)
            reduced = (load - contract_last(incoming, coupling_block)).astype(jnp.bfloat16)
            return contract_last(reduced, inverse_block).astype(jnp.bfloat16)

        def forward_waiting(unused):
            return outgoing

        result = lax.cond(valid, forward_active, forward_waiting, 0)
        solved = lax.dynamic_update_index_in_dim(solved, result, clipped, 0)
        return (solved, result)

    forward_start = (
        jnp.zeros((groups, width, order), jnp.bfloat16),
        jnp.zeros((width, order), jnp.bfloat16),
    )
    solved, forward_last = lax.fori_loop(0, moments, forward, forward_start)

    def backward(moment, carry):
        moved, outgoing = carry
        incoming = shifted(outgoing, "front", -1)
        panel = moment - (fronts - 1 - front_pos)
        valid = (panel >= 0) & (panel < groups)
        clipped = jnp.clip(panel, 0, groups - 1)

        def backward_active(unused):
            upper = lax.dynamic_index_in_dim(solved, clipped, 0, keepdims=False).astype(jnp.float32)
            reduced = (upper - incoming.astype(jnp.float32)).astype(jnp.bfloat16)
            displaced = jnp.dot(reduced, inverse_block, preferred_element_type=jnp.float32)
            handed = jnp.dot(
                displaced.astype(jnp.bfloat16), coupling_block, preferred_element_type=jnp.float32
            )
            return (displaced, handed.astype(jnp.bfloat16))

        def backward_waiting(unused):
            return (lax.dynamic_index_in_dim(moved, clipped, 0, keepdims=False), outgoing)

        displaced, handed = lax.cond(valid, backward_active, backward_waiting, 0)
        moved = lax.dynamic_update_index_in_dim(moved, displaced, clipped, 0)
        return (moved, handed)

    backward_start = (
        jnp.zeros((groups, width, order), jnp.float32),
        jnp.zeros((width, order), jnp.bfloat16),
    )
    moved, backward_last = lax.fori_loop(0, moments, backward, backward_start)
    displacement = moved.reshape(columns_all, order)
    modal = lax.psum(
        contract_last(displacement.astype(jnp.bfloat16), mode_block).astype(jnp.bfloat16), "front"
    )
    deflated = displacement - jnp.dot(modal, mode_block, preferred_element_type=jnp.float32)
    own_rows = jnp.take(deflated, offsets, axis=1).T
    total_ids = interface_id.shape[0] * columns_all // 2
    dual_ids = jnp.arange(total_ids, dtype=jnp.int32)
    owners = lax.axis_size("sub") * fronts
    share = total_ids // owners
    gathered = lax.all_gather(
        own_rows.astype(jnp.bfloat16), ("sub", "front"), axis=0, tiled=True
    ).astype(own_rows.dtype)
    subs_all = interface_id.shape[0]
    flat_labels = interface_id.reshape(-1)
    owner_pos = sub_pos * fronts + front_pos
    targets = owner_pos * share + jnp.arange(share, dtype=jnp.int32)
    row_select = (targets[:, None] == flat_labels[None, :]).astype(jnp.float32)
    reduced = jnp.einsum(
        "asc,scd->asd",
        row_select.reshape(share, subs_all, columns_all),
        gathered.reshape(subs_all, columns_all, columns_all),
        precision=lax.Precision.HIGHEST,
    )
    column_place = (flat_labels[:, None] == dual_ids[None, :]).astype(jnp.float32)
    flexibility = jnp.dot(
        reduced.reshape(share, subs_all * columns_all),
        column_place,
        precision=lax.Precision.HIGHEST,
    )
    return (deflated.astype(jnp.bfloat16)[None], flexibility)


def solution(mesh):
    return jax.shard_map(
        on_device,
        mesh=mesh,
        in_specs=(
            P("sub", "front", None),
            P("sub", "front", None),
            P("sub", None, "front"),
            P("sub", "front"),
            P(),
        ),
        out_specs=(P("sub", None, "front"), P(("sub", "front"), None)),
        check_vma=False,
    )
```

profile of v0, /device:TPU:0, one launch (start us, length us, event | category | flops | bytes accessed | tf_op | source)
XLA Modules:
  0.0 390.6 jit_solution(3004368580467127556)
XLA Ops:
  7.3 2.6 convolution_bitcast_fusion
  9.8 0.1 broadcast.48.clone
  9.9 126.6 %while.35 = (s32[]{:T(128)}, bf16[1,256,2048]{2,1,0:T(8,128)(2,1)}, bf16[256,2048]{1,0:T(8,128)(2,1)S(1)}, s32[]{:T(128)}, f32[1,256,2048]{2,1,0:T(8,128)}, /*in...) while((s32[]{:T(128)}, bf16[1,256,2048]{2,1,0:T(8,128)(2,1)}, ...), condition=%wide.region_3.4_spmd, body=%wide.region_0.3_spmd.sunk | while | flops 4296540160 | bytes 33554672 | solution.py:66
  10.0 0.1 copy.23
  10.1 5.0 %collective-permute-start = (bf16[256,2048]{1,0:T(8,128)(2,1)S(1)}, bf16[256,2048]{1,0:T(8,128)(2,1)S(1)}, u32[]{:S(2)}, u32[]{:S(2)}) collective-permute-start(bf16[256,2048]{1,0:T(8,128)(2,1)S(1)} %copy.23), channel_id=1, source_target_pairs={{0,1},{1,2},{2,3},{4,5},{5,6},{6,7},{8,9},{9,10},{10,11},{12,13},{... | collective-permute-start | bytes 3145736 | tf_op jit(solution)/shard_map/while/body/eval_jaxpr/ppermute | solution.py:10
  15.1 22.3 %collective-permute-done = bf16[256,2048]{1,0:T(8,128)(2,1)S(1)} collective-permute-done((bf16[256,2048]{1,0:T(8,128)(2,1)S(1)}, bf16[256,2048]{1,0:T(8,128)(2,1)S(1)}, u32[]{:S(2)}, u32[]{:S(2)}) %collective-permute-start) | collective-permute-done | bytes 1048608 | tf_op jit(solution)/shard_map/while/body/eval_jaxpr/ppermute | solution.py:10
  37.4 10.9 %conditional.4 = (bf16[256,2048]{1,0:T(8,128)(2,1)S(1)}) conditional(s32[]{:T(128)} %convert_element_type.98, bf16[256,2048]{1,0:T(8,128)(2,1)S(1)} %copy.23, (f32[1,256,2048]{2,1,0:T(8,128)}, bf16[256,2048]{1,0:T(8,128)(2,1)S(1)}, bf16[2048,2048]{1,0:T(8,128)(2,1)}, bf16[2048,2048]{1,0:T(8,128)(2,1)}) %tuple.101), branch_computations={%region_1.1_spmd, %region_2.2_spmd} | conditional | flops 4296540160 | bytes 20971528 | solution.py:58
  37.4 10.9 %convolution_convert_fusion = bf16[256,2048]{1,0:T(8,128)(2,1)S(1)} fusion(bf16[2048,2048]{1,0:T(8,128)(2,1)} %get-tuple-element.340, bf16[256,2048]{1,0:T(8,128)(2,1)S(1)} %get-tuple-element.338, bf16[2048,2048]{1,0:T(8,128)(2,1)} %get-tuple-element.339, f32[1,256,2048]{2,1,0:T(8,128)} %get-tuple-element.337), kind=kOutput, calls=%fused_computation.3 | convolution fusion | flops 4296540160 | bytes 20971520 | tf_op jit(solution)/shard_map/while/body/eval_jaxpr/cond/branch_1_fun/dot_general | solution.py:14
  48.4 0.1 copy.26
  48.5 0.9 copy-done.1
  49.3 0.1 copy.23
  49.4 1.4 collective-permute-start
  50.8 21.8 %collective-permute-done = bf16[256,2048]{1,0:T(8,128)(2,1)S(1)} collective-permute-done((bf16[256,2048]{1,0:T(8,128)(2,1)S(1)}, bf16[256,2048]{1,0:T(8,128)(2,1)S(1)}, u32[]{:S(2)}, u32[]{:S(2)}) %collective-permute-start) | collective-permute-done | bytes 1048608 | tf_op jit(solution)/shard_map/while/body/eval_jaxpr/ppermute | solution.py:10
  72.6 0.1 copy.26
  72.7 0.9 copy-done.1
  73.5 0.1 copy.23
  73.6 15.4 %collective-permute-start = (bf16[256,2048]{1,0:T(8,128)(2,1)S(1)}, bf16[256,2048]{1,0:T(8,128)(2,1)S(1)}, u32[]{:S(2)}, u32[]{:S(2)}) collective-permute-start(bf16[256,2048]{1,0:T(8,128)(2,1)S(1)} %copy.23), channel_id=1, source_target_pairs={{0,1},{1,2},{2,3},{4,5},{5,6},{6,7},{8,9},{9,10},{10,11},{12,13},{... | collective-permute-start | bytes 3145736 | tf_op jit(solution)/shard_map/while/body/eval_jaxpr/ppermute | solution.py:10
  89.1 20.9 %collective-permute-done = bf16[256,2048]{1,0:T(8,128)(2,1)S(1)} collective-permute-done((bf16[256,2048]{1,0:T(8,128)(2,1)S(1)}, bf16[256,2048]{1,0:T(8,128)(2,1)S(1)}, u32[]{:S(2)}, u32[]{:S(2)}) %collective-permute-start) | collective-permute-done | bytes 1048608 | tf_op jit(solution)/shard_map/while/body/eval_jaxpr/ppermute | solution.py:10
  110.0 0.1 copy.26
  110.1 0.9 copy-done.1
  110.9 0.1 copy.23
  111.0 4.5 %collective-permute-start = (bf16[256,2048]{1,0:T(8,128)(2,1)S(1)}, bf16[256,2048]{1,0:T(8,128)(2,1)S(1)}, u32[]{:S(2)}, u32[]{:S(2)}) collective-permute-start(bf16[256,2048]{1,0:T(8,128)(2,1)S(1)} %copy.23), channel_id=1, source_target_pairs={{0,1},{1,2},{2,3},{4,5},{5,6},{6,7},{8,9},{9,10},{10,11},{12,13},{... | collective-permute-start | bytes 3145736 | tf_op jit(solution)/shard_map/while/body/eval_jaxpr/ppermute | solution.py:10
  115.5 20.0 %collective-permute-done = bf16[256,2048]{1,0:T(8,128)(2,1)S(1)} collective-permute-done((bf16[256,2048]{1,0:T(8,128)(2,1)S(1)}, bf16[256,2048]{1,0:T(8,128)(2,1)S(1)}, u32[]{:S(2)}, u32[]{:S(2)}) %collective-permute-start) | collective-permute-done | bytes 1048608 | tf_op jit(solution)/shard_map/while/body/eval_jaxpr/ppermute | solution.py:10
  135.6 0.9 copy-done.1
  136.5 1.6 broadcast_in_dim.49
  138.1 0.1 broadcast.48
  138.2 144.6 %while.36 = (s32[]{:T(128)}, f32[1,256,2048]{2,1,0:T(8,128)}, bf16[256,2048]{1,0:T(8,128)(2,1)S(1)}, s32[]{:T(128)}, bf16[1,256,2048]{2,1,0:T(8,128)(2,1)S(1)}, ...) while((s32[]{:T(128)}, f32[1,256,2048]{2,1,0:T(8,128)}, ...), condition=%wide.region_7.8_spmd, body=%wide.region_4.7_spmd.sunk | while | flops 4298113024 | bytes 70254888 | solution.py:95
  138.2 1.3 collective-permute-start.1
  139.5 32.5 %collective-permute-done.1 = bf16[256,2048]{1,0:T(8,128)(2,1)} collective-permute-done((bf16[256,2048]{1,0:T(8,128)(2,1)S(1)}, bf16[256,2048]{1,0:T(8,128)(2,1)}, u32[]{:S(2)}, u32[]{:S(2)}) %collective-permute-start.1) | collective-permute-done | bytes 1048608 | tf_op jit(solution)/shard_map/while/body/eval_jaxpr/ppermute | solution.py:10
  172.1 1.3 collective-permute-start.1
  173.4 22.9 %collective-permute-done.1 = bf16[256,2048]{1,0:T(8,128)(2,1)} collective-permute-done((bf16[256,2048]{1,0:T(8,128)(2,1)S(1)}, bf16[256,2048]{1,0:T(8,128)(2,1)}, u32[]{:S(2)}, u32[]{:S(2)}) %collective-permute-start.1) | collective-permute-done | bytes 1048608 | tf_op jit(solution)/shard_map/while/body/eval_jaxpr/ppermute | solution.py:10
  196.3 1.3 collective-permute-start.1
  197.5 31.3 %collective-permute-done.1 = bf16[256,2048]{1,0:T(8,128)(2,1)} collective-permute-done((bf16[256,2048]{1,0:T(8,128)(2,1)S(1)}, bf16[256,2048]{1,0:T(8,128)(2,1)}, u32[]{:S(2)}, u32[]{:S(2)}) %collective-permute-start.1) | collective-permute-done | bytes 1048608 | tf_op jit(solution)/shard_map/while/body/eval_jaxpr/ppermute | solution.py:10
  228.8 1.3 collective-permute-start.1
  230.1 44.1 %collective-permute-done.1 = bf16[256,2048]{1,0:T(8,128)(2,1)} collective-permute-done((bf16[256,2048]{1,0:T(8,128)(2,1)S(1)}, bf16[256,2048]{1,0:T(8,128)(2,1)}, u32[]{:S(2)}, u32[]{:S(2)}) %collective-permute-start.1) | collective-permute-done | bytes 1048608 | tf_op jit(solution)/shard_map/while/body/eval_jaxpr/ppermute | solution.py:10
  274.2 8.5 %conditional.5 = ((bf16[256,2048]{1,0:T(8,128)(2,1)S(1)}, f32[1,256,2048]{2,1,0:T(8,128)})) conditional(s32[]{:T(128)} %convert_element_type.99, (bf16[256,2048]{1,0:T(8,128)(2,1)S(1)}, f32[1,256,2048]{2,1,0:T(8,128)}) %tuple.103, (bf16[1,256,2048]{2,1,0:T(8,128)(2,1)S(1)}, bf16[256,2048]{1,0:T(8,128)(2,1)}, bf16[2048,2048]{1,0:T(8,128)(2,1)}, ...), branch_computations={%region_5.5_spmd, %region_6.6_spmd} | conditional | flops 4298113024 | bytes 66060368 | solution.py:87
  274.2 6.2 %fusion.2 = f32[256,2048]{1,0:T(8,128)S(1)} fusion(bf16[2048,2048]{1,0:T(8,128)(2,1)} %get-tuple-element.350, bf16[256,2048]{1,0:T(8,128)(2,1)} %get-tuple-element.349, bf16[1,256,2048]{2,1,0:T(8,128)(2,1)S(1)} %get-tuple-element.348), kind=kOutput, calls=%fused_computation.7 | convolution fusion | flops 2149580800 | bytes 12582912 | tf_op jit(solution)/shard_map/while/body/eval_jaxpr/cond/branch_1_fun/dot_general | solution.py:78
  280.4 2.3 convolution_convert_fusion.1
  282.8 3.1 fusion.11
  286.0 0.2 all-gather.2.cloned.1.call-start
  286.3 33.1 %all-reduce.2.cloned.1.call-done = bf16[256,300]{1,0:T(8,128)(2,1)} async-done(((bf16[256,300]{1,0:T(8,128)(2,1)}), bf16[256,300]{1,0:T(8,128)(2,1)}) %all-reduce.2.cloned.1.call-update) | async-done | bytes 153616 | tf_op jit(solution)/shard_map/psum | solution.py:97
  319.4 2.6 convolution_subtract_fusion.1
  322.0 1.5 copy.8
  323.5 0.7 gather_fusion
  324.2 0.7 select_convert_fusion
  324.9 53.6 %all-gather.2.cloned.1.call-done = bf16[2048,256]{1,0:T(8,128)(2,1)} async-done(((bf16[64,256]{1,0:T(8,128)(2,1)}), bf16[2048,256]{1,0:T(8,128)(2,1)}) %all-gather.2.cloned.1.call-update) | async-done | bytes 1048592 | tf_op jit(solution)/shard_map/all_gather | solution.py:106
  378.5 1.5 convolution_bitcast_fusion.1
  380.1 3.8 fusion.6
  (36 shorter events, 0.3 us)
Async XLA Ops:
  7.2 275.7 %copy-start = (bf16[1,300,2048]{2,1,0:T(8,128)(2,1)S(1)}, bf16[1,300,2048]{2,1,0:T(8,128)(2,1)}, u32[]{:S(2)}) copy-start(bf16[1,300,2048]{2,1,0:T(8,128)(2,1)} %param.15) | copy-start | bytes 3686404
  7.2 312.2 %all-reduce.2.cloned.1.call-start = ((), (), s32[]{:S(2)}) async-start(), calls=%async_computation | async-start | bytes 393216 | tf_op jit(solution)/shard_map/psum | solution.py:97
  10.1 27.4 %collective-permute-start = (bf16[256,2048]{1,0:T(8,128)(2,1)S(1)}, bf16[256,2048]{1,0:T(8,128)(2,1)S(1)}, u32[]{:S(2)}, u32[]{:S(2)}) collective-permute-start(bf16[256,2048]{1,0:T(8,128)(2,1)S(1)} %copy.23), channel_id=1, source_target_pairs={{0,1},{1,2},{2,3},{4,5},{5,6},{6,7},{8,9},{9,10},{10,11},{12,13},{... | collective-permute-start | bytes 3145736 | tf_op jit(solution)/shard_map/while/body/eval_jaxpr/ppermute | solution.py:10
  48.4 1.0 copy-start.1
  49.4 23.1 %collective-permute-start = (bf16[256,2048]{1,0:T(8,128)(2,1)S(1)}, bf16[256,2048]{1,0:T(8,128)(2,1)S(1)}, u32[]{:S(2)}, u32[]{:S(2)}) collective-permute-start(bf16[256,2048]{1,0:T(8,128)(2,1)S(1)} %copy.23), channel_id=1, source_target_pairs={{0,1},{1,2},{2,3},{4,5},{5,6},{6,7},{8,9},{9,10},{10,11},{12,13},{... | collective-permute-start | bytes 3145736 | tf_op jit(solution)/shard_map/while/body/eval_jaxpr/ppermute | solution.py:10
  72.6 1.0 copy-start.1
  73.6 36.3 %collective-permute-start = (bf16[256,2048]{1,0:T(8,128)(2,1)S(1)}, bf16[256,2048]{1,0:T(8,128)(2,1)S(1)}, u32[]{:S(2)}, u32[]{:S(2)}) collective-permute-start(bf16[256,2048]{1,0:T(8,128)(2,1)S(1)} %copy.23), channel_id=1, source_target_pairs={{0,1},{1,2},{2,3},{4,5},{5,6},{6,7},{8,9},{9,10},{10,11},{12,13},{... | collective-permute-start | bytes 3145736 | tf_op jit(solution)/shard_map/while/body/eval_jaxpr/ppermute | solution.py:10
  110.0 1.0 copy-start.1
  111.0 24.5 %collective-permute-start = (bf16[256,2048]{1,0:T(8,128)(2,1)S(1)}, bf16[256,2048]{1,0:T(8,128)(2,1)S(1)}, u32[]{:S(2)}, u32[]{:S(2)}) collective-permute-start(bf16[256,2048]{1,0:T(8,128)(2,1)S(1)} %copy.23), channel_id=1, source_target_pairs={{0,1},{1,2},{2,3},{4,5},{5,6},{6,7},{8,9},{9,10},{10,11},{12,13},{... | collective-permute-start | bytes 3145736 | tf_op jit(solution)/shard_map/while/body/eval_jaxpr/ppermute | solution.py:10
  135.5 1.0 copy-start.1
  136.5 1.7 copy-start.2
  138.2 33.8 %collective-permute-start.1 = (bf16[256,2048]{1,0:T(8,128)(2,1)S(1)}, bf16[256,2048]{1,0:T(8,128)(2,1)}, u32[]{:S(2)}, u32[]{:S(2)}) collective-permute-start(bf16[256,2048]{1,0:T(8,128)(2,1)S(1)} %get-tuple-element.526), channel_id=1, source_target_pairs={{1,0},{2,1},{3,2},{5,4},{6,5},{7,6},{9,8},{10,9},{11,10},{13,12},{... | collective-permute-start | bytes 3145736 | tf_op jit(solution)/shard_map/while/body/eval_jaxpr/ppermute | solution.py:10
  172.1 24.2 %collective-permute-start.1 = (bf16[256,2048]{1,0:T(8,128)(2,1)S(1)}, bf16[256,2048]{1,0:T(8,128)(2,1)}, u32[]{:S(2)}, u32[]{:S(2)}) collective-permute-start(bf16[256,2048]{1,0:T(8,128)(2,1)S(1)} %get-tuple-element.526), channel_id=1, source_target_pairs={{1,0},{2,1},{3,2},{5,4},{6,5},{7,6},{9,8},{10,9},{11,10},{13,12},{... | collective-permute-start | bytes 3145736 | tf_op jit(solution)/shard_map/while/body/eval_jaxpr/ppermute | solution.py:10
  196.3 32.6 %collective-permute-start.1 = (bf16[256,2048]{1,0:T(8,128)(2,1)S(1)}, bf16[256,2048]{1,0:T(8,128)(2,1)}, u32[]{:S(2)}, u32[]{:S(2)}) collective-permute-start(bf16[256,2048]{1,0:T(8,128)(2,1)S(1)} %get-tuple-element.526), channel_id=1, source_target_pairs={{1,0},{2,1},{3,2},{5,4},{6,5},{7,6},{9,8},{10,9},{11,10},{13,12},{... | collective-permute-start | bytes 3145736 | tf_op jit(solution)/shard_map/while/body/eval_jaxpr/ppermute | solution.py:10
  228.8 45.4 %collective-permute-start.1 = (bf16[256,2048]{1,0:T(8,128)(2,1)S(1)}, bf16[256,2048]{1,0:T(8,128)(2,1)}, u32[]{:S(2)}, u32[]{:S(2)}) collective-permute-start(bf16[256,2048]{1,0:T(8,128)(2,1)S(1)} %get-tuple-element.526), channel_id=1, source_target_pairs={{1,0},{2,1},{3,2},{5,4},{6,5},{7,6},{9,8},{10,9},{11,10},{13,12},{... | collective-permute-start | bytes 3145736 | tf_op jit(solution)/shard_map/while/body/eval_jaxpr/ppermute | solution.py:10
  274.2 6.2 %copy-start.7 = (bf16[2048,2048]{1,0:T(8,128)(2,1)S(1)}, bf16[2048,2048]{1,0:T(8,128)(2,1)}, u32[]{:S(2)}) copy-start(bf16[2048,2048]{1,0:T(8,128)(2,1)} %get-tuple-element.351) | copy-start | bytes 25165828 | tf_op jit(solution)/shard_map/while/body/eval_jaxpr/cond
  280.4 2.4 copy-start.3
  282.8 3.4 copy-start.6
  282.8 36.5 %copy-start.4 = (f32[1,256,2048]{2,1,0:T(8,128)S(1)}, f32[1,256,2048]{2,1,0:T(8,128)}, u32[]{:S(2)}) copy-start(f32[1,256,2048]{2,1,0:T(8,128)} %get-tuple-element.367) | copy-start | bytes 6291460
  286.0 92.5 %all-gather.2.cloned.1.call-start = ((), (), s32[]{:S(2)}) async-start(), calls=%async_computation.1 | async-start | bytes 1081344 | tf_op jit(solution)/shard_map/all_gather | solution.py:106
  322.0 2.9 copy-start.5
Sparse Core Ops, SparseCore 0:
  286.1 33.1 all-reduce.1
  325.0 53.4 all-gather.1
where the time goes:
time: 391 us
  waiting for transfers between devices  302 us (77%)
  matrix products  33 us (8%)
  starting transfers between devices  31.6 us (8%)
  between operations  14.2 us (4%)
  local copies, waits for them, and re-layouts  8.29 us (2%)
    ppermute x8, waiting for transfers between devices, shifted(): lax.ppermute(value, axis, [(source, source + steps) for source in range(l...  216 us
    all_gather x1, waiting for transfers between devices, on_device(): lax.all_gather(own_rows.astype(jnp.bfloat16), ('sub', 'front'), axis=0, t...  53.6 us
    psum x1, waiting for transfers between devices, on_device(): lax.psum(contract_last(displacement.astype(jnp.bfloat16), mode_block).ast...  33.1 us
    ppermute x8, starting transfers between devices, shifted(): lax.ppermute(value, axis, [(source, source + steps) for source in range(l...  31.4 us
    dot_general x2, matrix products, contract_last(): lax.dot_general(left, right, (((1,), (1,)), ((), ())), preferred_element_...  14.1 us
  transfers between devices with their start and end apart: 10, of which 10 were waited for; matrix products, arithmetic and copies ran while one was open for 0% of the time, Pallas kernels for 0%

commit v1 on v0

--- a/solution.py
+++ b/solution.py
@@ -2,6 +2,7 @@
 import jax.numpy as jnp
 from jax import lax
 from jax.sharding import PartitionSpec as P
+from jax.lax import axis_index, ppermute, psum
 
 
 def shifted(value, axis, steps):
@@ -103,9 +104,23 @@
     dual_ids = jnp.arange(total_ids, dtype=jnp.int32)
     owners = lax.axis_size("sub") * fronts
     share = total_ids // owners
-    gathered = lax.all_gather(
-        own_rows.astype(jnp.bfloat16), ("sub", "front"), axis=0, tiled=True
-    ).astype(own_rows.dtype)
+
+    def attach_bands_over_axis(here_x, dim_k):
+        block_next = psum(1, axis_name=("sub", "front"))
+        g_now = axis_index(("sub", "front"))
+        x_next, near, extra = (block_next, g_now, here_x.shape[dim_k])
+        u1, x_new = (here_x, 1)
+        while x_new < x_next:
+            z_new = ppermute(
+                u1,
+                axis_name=("sub", "front"),
+                perm=[(kk, (kk - x_new) % x_next) for kk in range(x_next)],
+            )
+            u1 = jnp.concatenate([u1, z_new], axis=dim_k)
+            x_new = 2 * x_new
+        return jnp.roll(u1, near * extra, axis=dim_k)
+
+    gathered = attach_bands_over_axis(own_rows.astype(jnp.bfloat16), 0).astype(own_rows.dtype)
     subs_all = interface_id.shape[0]
     flat_labels = interface_id.reshape(-1)
     owner_pos = sub_pos * fronts + front_pos

time: 391 us -> 378 us (0.967)
  waiting for transfers between devices: 302 us -> 277 us
  local copies, waits for them, and re-layouts: 8.29 us -> 17.7 us
  starting transfers between devices: 31.6 us -> 36.2 us
    all_gather x1 -> x0, waiting for transfers between devices: 53.6 us -> none  [on_device(): lax.all_gather(own_rows.astype(jnp.bfloat16), ('sub', 'front'), axis=0, t...]
    ppermute x0 -> x5, waiting for transfers between devices: none -> 27.8 us  [attach_bands_over_axis(): ppermute(u1, axis_name=('sub', 'front'), perm=[(kk, (kk - x_new) % x_next...]
    unnamed x11 -> x21, local copies, waits for them, and re-layouts: 0.03 us -> 6.57 us
    ppermute x0 -> x5, starting transfers between devices: none -> 4.77 us  [attach_bands_over_axis(): ppermute(u1, axis_name=('sub', 'front'), perm=[(kk, (kk - x_new) % x_next...]
  transfers between devices with their start and end apart: 10 -> 14, of which waited for: 10 -> 14; matrix products, arithmetic and copies ran while one was open for 0% -> 1% of each run, Pallas kernels for 0% -> 0%
where the time goes in v1:
time: 378 us; the launch traced here: 377 us
  waiting for transfers between devices  277 us (73%)
  starting transfers between devices  36.2 us (10%)
  matrix products  31.8 us (8%)
  local copies, waits for them, and re-layouts  17.7 us (5%)
  between operations  14.2 us (4%)
    ppermute x8, waiting for transfers between devices, shifted(): lax.ppermute(value, axis, [(source, source + steps) for source in range(l...  216 us
    psum x1, waiting for transfers between devices, on_device(): lax.psum(contract_last(displacement.astype(jnp.bfloat16), mode_block).ast...  33.3 us
    ppermute x8, starting transfers between devices, shifted(): lax.ppermute(value, axis, [(source, source + steps) for source in range(l...  31.4 us
    ppermute x5, waiting for transfers between devices, attach_bands_over_axis(): ppermute(u1, axis_name=('sub', 'front'), perm=[(kk, (kk - x_new) % x_next...  27.8 us
    dot_general x2, matrix products, contract_last(): lax.dot_general(left, right, (((1,), (1,)), ((), ())), preferred_element_...  14.1 us
  transfers between devices with their start and end apart: 14, of which 14 were waited for; matrix products, arithmetic and copies ran while one was open for 1% of the time, Pallas kernels for 0%

profile of v1, /device:TPU:0, one launch (start us, length us, event | category | flops | bytes accessed | tf_op | source)
XLA Modules:
  0.0 377.2 jit_solution(18032869375030888668)
XLA Ops:
  7.3 2.6 convolution_bitcast_fusion
  9.9 126.6 %while.35 = (s32[]{:T(128)}, bf16[1,256,2048]{2,1,0:T(8,128)(2,1)}, bf16[256,2048]{1,0:T(8,128)(2,1)S(1)}, s32[]{:T(128)}, f32[1,256,2048]{2,1,0:T(8,128)}, /*in...) while((s32[]{:T(128)}, bf16[1,256,2048]{2,1,0:T(8,128)(2,1)}, ...), condition=%wide.region_3.4_spmd, body=%wide.region_0.3_spmd.sunk | while | flops 4296540160 | bytes 33554672 | solution.py:67
  10.1 5.0 %collective-permute-start = (bf16[256,2048]{1,0:T(8,128)(2,1)S(1)}, bf16[256,2048]{1,0:T(8,128)(2,1)S(1)}, u32[]{:S(2)}, u32[]{:S(2)}) collective-permute-start(bf16[256,2048]{1,0:T(8,128)(2,1)S(1)} %copy.23), channel_id=1, source_target_pairs={{0,1},{1,2},{2,3},{4,5},{5,6},{6,7},{8,9},{9,10},{10,11},{12,13},{... | collective-permute-start | bytes 3145736 | tf_op jit(solution)/shard_map/while/body/eval_jaxpr/ppermute | solution.py:11
  15.1 22.3 %collective-permute-done = bf16[256,2048]{1,0:T(8,128)(2,1)S(1)} collective-permute-done((bf16[256,2048]{1,0:T(8,128)(2,1)S(1)}, bf16[256,2048]{1,0:T(8,128)(2,1)S(1)}, u32[]{:S(2)}, u32[]{:S(2)}) %collective-permute-start) | collective-permute-done | bytes 1048608 | tf_op jit(solution)/shard_map/while/body/eval_jaxpr/ppermute | solution.py:11
  37.4 10.9 %conditional.4 = (bf16[256,2048]{1,0:T(8,128)(2,1)S(1)}) conditional(s32[]{:T(128)} %convert_element_type.98, bf16[256,2048]{1,0:T(8,128)(2,1)S(1)} %copy.23, (f32[1,256,2048]{2,1,0:T(8,128)}, bf16[256,2048]{1,0:T(8,128)(2,1)S(1)}, bf16[2048,2048]{1,0:T(8,128)(2,1)}, bf16[2048,2048]{1,0:T(8,128)(2,1)}) %tuple.106), branch_computations={%region_1.1_spmd, %region_2.2_spmd} | conditional | flops 4296540160 | bytes 20971528 | solution.py:59
  37.4 10.9 %convolution_convert_fusion = bf16[256,2048]{1,0:T(8,128)(2,1)S(1)} fusion(bf16[2048,2048]{1,0:T(8,128)(2,1)} %get-tuple-element.340, bf16[256,2048]{1,0:T(8,128)(2,1)S(1)} %get-tuple-element.338, bf16[2048,2048]{1,0:T(8,128)(2,1)} %get-tuple-element.339, f32[1,256,2048]{2,1,0:T(8,128)} %get-tuple-element.337), kind=kOutput, calls=%fused_computation.3 | convolution fusion | flops 4296540160 | bytes 20971520 | tf_op jit(solution)/shard_map/while/body/eval_jaxpr/cond/branch_1_fun/dot_general | solution.py:15
  48.5 0.9 copy-done.1
  49.4 1.4 collective-permute-start
  50.8 21.8 %collective-permute-done = bf16[256,2048]{1,0:T(8,128)(2,1)S(1)} collective-permute-done((bf16[256,2048]{1,0:T(8,128)(2,1)S(1)}, bf16[256,2048]{1,0:T(8,128)(2,1)S(1)}, u32[]{:S(2)}, u32[]{:S(2)}) %collective-permute-start) | collective-permute-done | bytes 1048608 | tf_op jit(solution)/shard_map/while/body/eval_jaxpr/ppermute | solution.py:11
  72.7 0.9 copy-done.1
  73.6 15.4 %collective-permute-start = (bf16[256,2048]{1,0:T(8,128)(2,1)S(1)}, bf16[256,2048]{1,0:T(8,128)(2,1)S(1)}, u32[]{:S(2)}, u32[]{:S(2)}) collective-permute-start(bf16[256,2048]{1,0:T(8,128)(2,1)S(1)} %copy.23), channel_id=1, source_target_pairs={{0,1},{1,2},{2,3},{4,5},{5,6},{6,7},{8,9},{9,10},{10,11},{12,13},{... | collective-permute-start | bytes 3145736 | tf_op jit(solution)/shard_map/while/body/eval_jaxpr/ppermute | solution.py:11
  89.1 20.9 %collective-permute-done = bf16[256,2048]{1,0:T(8,128)(2,1)S(1)} collective-permute-done((bf16[256,2048]{1,0:T(8,128)(2,1)S(1)}, bf16[256,2048]{1,0:T(8,128)(2,1)S(1)}, u32[]{:S(2)}, u32[]{:S(2)}) %collective-permute-start) | collective-permute-done | bytes 1048608 | tf_op jit(solution)/shard_map/while/body/eval_jaxpr/ppermute | solution.py:11
  110.1 0.9 copy-done.1
  111.0 4.5 %collective-permute-start = (bf16[256,2048]{1,0:T(8,128)(2,1)S(1)}, bf16[256,2048]{1,0:T(8,128)(2,1)S(1)}, u32[]{:S(2)}, u32[]{:S(2)}) collective-permute-start(bf16[256,2048]{1,0:T(8,128)(2,1)S(1)} %copy.23), channel_id=1, source_target_pairs={{0,1},{1,2},{2,3},{4,5},{5,6},{6,7},{8,9},{9,10},{10,11},{12,13},{... | collective-permute-start | bytes 3145736 | tf_op jit(solution)/shard_map/while/body/eval_jaxpr/ppermute | solution.py:11
  115.5 20.0 %collective-permute-done = bf16[256,2048]{1,0:T(8,128)(2,1)S(1)} collective-permute-done((bf16[256,2048]{1,0:T(8,128)(2,1)S(1)}, bf16[256,2048]{1,0:T(8,128)(2,1)S(1)}, u32[]{:S(2)}, u32[]{:S(2)}) %collective-permute-start) | collective-permute-done | bytes 1048608 | tf_op jit(solution)/shard_map/while/body/eval_jaxpr/ppermute | solution.py:11
  135.6 0.9 copy-done.1
  136.5 1.6 broadcast_in_dim.49
  138.2 144.6 %while.36 = (s32[]{:T(128)}, f32[1,256,2048]{2,1,0:T(8,128)}, bf16[256,2048]{1,0:T(8,128)(2,1)S(1)}, s32[]{:T(128)}, bf16[1,256,2048]{2,1,0:T(8,128)(2,1)S(1)}, ...) while((s32[]{:T(128)}, f32[1,256,2048]{2,1,0:T(8,128)}, ...), condition=%wide.region_7.8_spmd, body=%wide.region_4.7_spmd.sunk | while | flops 4298113024 | bytes 70254888 | solution.py:96
  138.2 1.3 collective-permute-start.1
  139.5 32.5 %collective-permute-done.1 = bf16[256,2048]{1,0:T(8,128)(2,1)} collective-permute-done((bf16[256,2048]{1,0:T(8,128)(2,1)S(1)}, bf16[256,2048]{1,0:T(8,128)(2,1)}, u32[]{:S(2)}, u32[]{:S(2)}) %collective-permute-start.1) | collective-permute-done | bytes 1048608 | tf_op jit(solution)/shard_map/while/body/eval_jaxpr/ppermute | solution.py:11
  172.0 1.3 collective-permute-start.1
  173.3 22.9 %collective-permute-done.1 = bf16[256,2048]{1,0:T(8,128)(2,1)} collective-permute-done((bf16[256,2048]{1,0:T(8,128)(2,1)S(1)}, bf16[256,2048]{1,0:T(8,128)(2,1)}, u32[]{:S(2)}, u32[]{:S(2)}) %collective-permute-start.1) | collective-permute-done | bytes 1048608 | tf_op jit(solution)/shard_map/while/body/eval_jaxpr/ppermute | solution.py:11
  196.2 1.3 collective-permute-start.1
  197.5 31.3 %collective-permute-done.1 = bf16[256,2048]{1,0:T(8,128)(2,1)} collective-permute-done((bf16[256,2048]{1,0:T(8,128)(2,1)S(1)}, bf16[256,2048]{1,0:T(8,128)(2,1)}, u32[]{:S(2)}, u32[]{:S(2)}) %collective-permute-start.1) | collective-permute-done | bytes 1048608 | tf_op jit(solution)/shard_map/while/body/eval_jaxpr/ppermute | solution.py:11
  228.8 1.3 collective-permute-start.1
  230.1 44.1 %collective-permute-done.1 = bf16[256,2048]{1,0:T(8,128)(2,1)} collective-permute-done((bf16[256,2048]{1,0:T(8,128)(2,1)S(1)}, bf16[256,2048]{1,0:T(8,128)(2,1)}, u32[]{:S(2)}, u32[]{:S(2)}) %collective-permute-start.1) | collective-permute-done | bytes 1048608 | tf_op jit(solution)/shard_map/while/body/eval_jaxpr/ppermute | solution.py:11
  274.2 8.5 %conditional.5 = ((bf16[256,2048]{1,0:T(8,128)(2,1)S(1)}, f32[1,256,2048]{2,1,0:T(8,128)})) conditional(s32[]{:T(128)} %convert_element_type.99, (bf16[256,2048]{1,0:T(8,128)(2,1)S(1)}, f32[1,256,2048]{2,1,0:T(8,128)}) %tuple.108, (bf16[1,256,2048]{2,1,0:T(8,128)(2,1)S(1)}, bf16[256,2048]{1,0:T(8,128)(2,1)}, bf16[2048,2048]{1,0:T(8,128)(2,1)}, ...), branch_computations={%region_5.5_spmd, %region_6.6_spmd} | conditional | flops 4298113024 | bytes 66060368 | solution.py:88
  274.2 6.2 %fusion.2 = f32[256,2048]{1,0:T(8,128)S(1)} fusion(bf16[2048,2048]{1,0:T(8,128)(2,1)} %get-tuple-element.350, bf16[256,2048]{1,0:T(8,128)(2,1)} %get-tuple-element.349, bf16[1,256,2048]{2,1,0:T(8,128)(2,1)S(1)} %get-tuple-element.348), kind=kOutput, calls=%fused_computation.7 | convolution fusion | flops 2149580800 | bytes 12582912 | tf_op jit(solution)/shard_map/while/body/eval_jaxpr/cond/branch_1_fun/dot_general | solution.py:79
  280.4 2.3 convolution_convert_fusion.1
  282.8 3.1 fusion.11
  286.0 33.3 %all-reduce.2.cloned.1.call-done = bf16[256,300]{1,0:T(8,128)(2,1)} async-done(((bf16[256,300]{1,0:T(8,128)(2,1)}), bf16[256,300]{1,0:T(8,128)(2,1)}) %all-reduce.2.cloned.1.call-update) | async-done | bytes 153616 | tf_op jit(solution)/shard_map/psum | solution.py:98
  319.3 2.6 convolution_subtract_fusion.1
  321.9 1.5 copy.8
  323.4 0.7 gather_fusion
  324.2 1.4 collective-permute-start.2
  325.6 2.6 collective-permute-done.2
  328.4 5.0 %collective-permute-done.3 = bf16[128,256]{1,0:T(8,128)(2,1)S(1)} collective-permute-done((bf16[128,256]{1,0:T(8,128)(2,1)S(1)}, bf16[128,256]{1,0:T(8,128)(2,1)S(1)}, u32[]{:S(2)}, u32[]{:S(2)}) %collective-permute-start.3) | collective-permute-done | bytes 65568 | tf_op jit(solution)/shard_map/ppermute | solution.py:114
  334.4 1.9 collective-permute-done.4
  336.3 2.5 collective-permute-start.5
  340.0 0.7 constant_dynamic-update-slice_fusion.1
  340.7 4.8 %collective-permute-done.5 = bf16[512,256]{1,0:T(8,128)(2,1)S(1)} collective-permute-done((bf16[512,256]{1,0:T(8,128)(2,1)S(1)}, bf16[512,256]{1,0:T(8,128)(2,1)S(1)}, u32[]{:S(2)}, u32[]{:S(2)}) %collective-permute-start.5) | collective-permute-done | bytes 262176 | tf_op jit(solution)/shard_map/ppermute | solution.py:114
  345.5 0.7 constant_dynamic-update-slice_fusion
  346.5 13.6 %collective-permute-done.6 = bf16[1024,256]{1,0:T(8,128)(2,1)S(1)} collective-permute-done((bf16[1024,256]{1,0:T(8,128)(2,1)S(1)}, bf16[1024,256]{1,0:T(8,128)(2,1)S(1)}, u32[]{:S(2)}, u32[]{:S(2)}) %collective-permute-start.6) | collective-permute-done | bytes 524320 | tf_op jit(solution)/shard_map/ppermute | solution.py:114
  360.1 0.8 constant_dynamic-update-slice_fusion.11
  363.4 0.7 constant_dynamic-update-slice_fusion.6
  364.2 0.8 constant_dynamic-update-slice_fusion.5
  365.0 1.3 constant_dynamic-slice_fusion
  366.6 3.8 fusion.6
  (59 shorter events, 6.8 us)
Async XLA Ops:
  7.2 275.6 %copy-start = (bf16[1,300,2048]{2,1,0:T(8,128)(2,1)S(1)}, bf16[1,300,2048]{2,1,0:T(8,128)(2,1)}, u32[]{:S(2)}) copy-start(bf16[1,300,2048]{2,1,0:T(8,128)(2,1)} %param.15) | copy-start | bytes 3686404
  7.2 312.1 %all-reduce.2.cloned.1.call-start = ((), (), s32[]{:S(2)}) async-start(), calls=%async_computation | async-start | bytes 393216 | tf_op jit(solution)/shard_map/psum | solution.py:98
  10.1 27.4 %collective-permute-start = (bf16[256,2048]{1,0:T(8,128)(2,1)S(1)}, bf16[256,2048]{1,0:T(8,128)(2,1)S(1)}, u32[]{:S(2)}, u32[]{:S(2)}) collective-permute-start(bf16[256,2048]{1,0:T(8,128)(2,1)S(1)} %copy.23), channel_id=1, source_target_pairs={{0,1},{1,2},{2,3},{4,5},{5,6},{6,7},{8,9},{9,10},{10,11},{12,13},{... | collective-permute-start | bytes 3145736 | tf_op jit(solution)/shard_map/while/body/eval_jaxpr/ppermute | solution.py:11
  48.4 1.0 copy-start.1
  49.4 23.1 %collective-permute-start = (bf16[256,2048]{1,0:T(8,128)(2,1)S(1)}, bf16[256,2048]{1,0:T(8,128)(2,1)S(1)}, u32[]{:S(2)}, u32[]{:S(2)}) collective-permute-start(bf16[256,2048]{1,0:T(8,128)(2,1)S(1)} %copy.23), channel_id=1, source_target_pairs={{0,1},{1,2},{2,3},{4,5},{5,6},{6,7},{8,9},{9,10},{10,11},{12,13},{... | collective-permute-start | bytes 3145736 | tf_op jit(solution)/shard_map/while/body/eval_jaxpr/ppermute | solution.py:11
  72.6 1.0 copy-start.1
  73.6 36.3 %collective-permute-start = (bf16[256,2048]{1,0:T(8,128)(2,1)S(1)}, bf16[256,2048]{1,0:T(8,128)(2,1)S(1)}, u32[]{:S(2)}, u32[]{:S(2)}) collective-permute-start(bf16[256,2048]{1,0:T(8,128)(2,1)S(1)} %copy.23), channel_id=1, source_target_pairs={{0,1},{1,2},{2,3},{4,5},{5,6},{6,7},{8,9},{9,10},{10,11},{12,13},{... | collective-permute-start | bytes 3145736 | tf_op jit(solution)/shard_map/while/body/eval_jaxpr/ppermute | solution.py:11
  109.9 1.0 copy-start.1
  111.0 24.5 %collective-permute-start = (bf16[256,2048]{1,0:T(8,128)(2,1)S(1)}, bf16[256,2048]{1,0:T(8,128)(2,1)S(1)}, u32[]{:S(2)}, u32[]{:S(2)}) collective-permute-start(bf16[256,2048]{1,0:T(8,128)(2,1)S(1)} %copy.23), channel_id=1, source_target_pairs={{0,1},{1,2},{2,3},{4,5},{5,6},{6,7},{8,9},{9,10},{10,11},{12,13},{... | collective-permute-start | bytes 3145736 | tf_op jit(solution)/shard_map/while/body/eval_jaxpr/ppermute | solution.py:11
  135.5 1.0 copy-start.1
  136.5 1.7 copy-start.2
  138.2 33.8 %collective-permute-start.1 = (bf16[256,2048]{1,0:T(8,128)(2,1)S(1)}, bf16[256,2048]{1,0:T(8,128)(2,1)}, u32[]{:S(2)}, u32[]{:S(2)}) collective-permute-start(bf16[256,2048]{1,0:T(8,128)(2,1)S(1)} %get-tuple-element.536), channel_id=1, source_target_pairs={{1,0},{2,1},{3,2},{5,4},{6,5},{7,6},{9,8},{10,9},{11,10},{13,12},{... | collective-permute-start | bytes 3145736 | tf_op jit(solution)/shard_map/while/body/eval_jaxpr/ppermute | solution.py:11
  172.0 24.2 %collective-permute-start.1 = (bf16[256,2048]{1,0:T(8,128)(2,1)S(1)}, bf16[256,2048]{1,0:T(8,128)(2,1)}, u32[]{:S(2)}, u32[]{:S(2)}) collective-permute-start(bf16[256,2048]{1,0:T(8,128)(2,1)S(1)} %get-tuple-element.536), channel_id=1, source_target_pairs={{1,0},{2,1},{3,2},{5,4},{6,5},{7,6},{9,8},{10,9},{11,10},{13,12},{... | collective-permute-start | bytes 3145736 | tf_op jit(solution)/shard_map/while/body/eval_jaxpr/ppermute | solution.py:11
  196.2 32.6 %collective-permute-start.1 = (bf16[256,2048]{1,0:T(8,128)(2,1)S(1)}, bf16[256,2048]{1,0:T(8,128)(2,1)}, u32[]{:S(2)}, u32[]{:S(2)}) collective-permute-start(bf16[256,2048]{1,0:T(8,128)(2,1)S(1)} %get-tuple-element.536), channel_id=1, source_target_pairs={{1,0},{2,1},{3,2},{5,4},{6,5},{7,6},{9,8},{10,9},{11,10},{13,12},{... | collective-permute-start | bytes 3145736 | tf_op jit(solution)/shard_map/while/body/eval_jaxpr/ppermute | solution.py:11
  228.8 45.4 %collective-permute-start.1 = (bf16[256,2048]{1,0:T(8,128)(2,1)S(1)}, bf16[256,2048]{1,0:T(8,128)(2,1)}, u32[]{:S(2)}, u32[]{:S(2)}) collective-permute-start(bf16[256,2048]{1,0:T(8,128)(2,1)S(1)} %get-tuple-element.536), channel_id=1, source_target_pairs={{1,0},{2,1},{3,2},{5,4},{6,5},{7,6},{9,8},{10,9},{11,10},{13,12},{... | collective-permute-start | bytes 3145736 | tf_op jit(solution)/shard_map/while/body/eval_jaxpr/ppermute | solution.py:11
  274.2 6.2 %copy-start.7 = (bf16[2048,2048]{1,0:T(8,128)(2,1)S(1)}, bf16[2048,2048]{1,0:T(8,128)(2,1)}, u32[]{:S(2)}) copy-start(bf16[2048,2048]{1,0:T(8,128)(2,1)} %get-tuple-element.351) | copy-start | bytes 25165828 | tf_op jit(solution)/shard_map/while/body/eval_jaxpr/cond
  280.4 2.4 copy-start.3
  282.8 3.2 copy-start.6
  282.8 36.5 %copy-start.4 = (f32[1,256,2048]{2,1,0:T(8,128)S(1)}, f32[1,256,2048]{2,1,0:T(8,128)}, u32[]{:S(2)}) copy-start(f32[1,256,2048]{2,1,0:T(8,128)} %get-tuple-element.367) | copy-start | bytes 6291460
  323.4 23.1 %copy-start.5 = (s32[8,256]{1,0:T(8,128)S(1)}, s32[8,256]{1,0:T(8,128)}, u32[]{:S(2)}) copy-start(s32[8,256]{1,0:T(8,128)} %param.17) | copy-start | bytes 24580
  324.2 4.0 %collective-permute-start.2 = (bf16[64,256]{1,0:T(8,128)(2,1)S(1)}, bf16[64,256]{1,0:T(8,128)(2,1)S(1)}, u32[]{:S(2)}, u32[]{:S(2)}) collective-permute-start(bf16[64,256]{1,0:T(8,128)(2,1)S(1)} %get-tuple-element.397), channel_id=1, source_target_pairs={{0,31},{1,0},{2,1},{3,2},{4,3},{5,4},{6,5},{7,6},{8,7},{9,8},{10,9... | collective-permute-start | bytes 98312 | tf_op jit(solution)/shard_map/ppermute | solution.py:114
  328.2 5.2 %collective-permute-start.3 = (bf16[128,256]{1,0:T(8,128)(2,1)S(1)}, bf16[128,256]{1,0:T(8,128)(2,1)S(1)}, u32[]{:S(2)}, u32[]{:S(2)}) collective-permute-start(bf16[128,256]{1,0:T(8,128)(2,1)S(1)} %pad_maximum_fusion.2), channel_id=1, source_target_pairs={{0,30},{1,31},{2,0},{3,1},{4,2},{5,3},{6,4},{7,5},{8,6},{9,7},{10,... | collective-permute-start | bytes 196616 | tf_op jit(solution)/shard_map/ppermute | solution.py:114
  333.4 2.9 collective-permute-start.4
  336.3 9.2 %collective-permute-start.5 = (bf16[512,256]{1,0:T(8,128)(2,1)S(1)}, bf16[512,256]{1,0:T(8,128)(2,1)S(1)}, u32[]{:S(2)}, u32[]{:S(2)}) collective-permute-start(bf16[512,256]{1,0:T(8,128)(2,1)S(1)} %pad_maximum_fusion), channel_id=1, source_target_pairs={{0,24},{1,25},{2,26},{3,27},{4,28},{5,29},{6,30},{7,31},{8,0},{9,1... | collective-permute-start | bytes 786440 | tf_op jit(solution)/shard_map/ppermute | solution.py:114
  346.2 13.9 %collective-permute-start.6 = (bf16[1024,256]{1,0:T(8,128)(2,1)S(1)}, bf16[1024,256]{1,0:T(8,128)(2,1)S(1)}, u32[]{:S(2)}, u32[]{:S(2)}) collective-permute-start(bf16[1024,256]{1,0:T(8,128)(2,1)S(1)} %get-tuple-element.398), channel_id=1, source_target_pairs={{0,16},{1,17},{2,18},{3,19},{4,20},{5,21},{6,22},{7,23},{8,24},{9,... | collective-permute-start | bytes 1572872 | tf_op jit(solution)/shard_map/ppermute | solution.py:114
Sparse Core Ops, SparseCore 0:
  286.1 33.1 all-reduce.1
